TPU v7x, 128 devices: a whole 4x4x4 slice. The times are simulated.
128 devices in a mesh: dp: 2 (over core), lat: 8 (over z, y_hi), lon: 8 (over y_lo, x).
Axes of the slice: x: 4, y: 4 (y_hi: 2, y_lo: 2; y = y_hi * 2 + y_lo), z: 4, core: 2. Of those that a mesh axis runs over, the one named last changes fastest.
Arguments:
- fields: bfloat16 [2, 640, 1024, 128], P('dp', 'lat', 'lon'), may hold values from -6 to 6
- down_weight: bfloat16 [3, 3, 128, 128], P(None, None, 'dp'), may hold values from -0.1875 to 0.1875
- mid_weight: bfloat16 [3, 3, 128, 128], P(None, None, 'dp'), may hold values from -0.1875 to 0.1875
- up_weight: bfloat16 [3, 3, 128, 128], P(None, None, 'dp'), may hold values from -0.1875 to 0.1875
- cotangent: bfloat16 [2, 640, 1024, 128], P('dp', 'lat', 'lon'), may hold values from -6 to 6
Outputs:
- level_out: bfloat16 [2, 640, 1024, 128], P('dp', 'lat', 'lon')
- grad_fields: bfloat16 [2, 640, 1024, 128], P('dp', 'lat', 'lon')
- grad_down: float32 [3, 3, 128, 128], P(None, None, 'dp')
- grad_mid: float32 [3, 3, 128, 128], P(None, None, 'dp')
- grad_up: float32 [3, 3, 128, 128], P(None, None, 'dp')
All inputs are finite; a program needn't handle non-finite values.
Results may differ from a plain program's by a relative error of at most 0.012.
Values may be sent and summed in bfloat16 or wider, within the bound.
No kernel may reach another device: no remote copies, remote signals or barrier semaphores. Data moves between devices by JAX's collectives and lax.ppermute only.
A program may use at most 128 MiB of HBM per device.

v0:
```python
import math
import jax
import jax.numpy as jnp
from jax import lax
from jax.sharding import PartitionSpec as P


def extended(block, sides, width, periodic):
    for axis, dim in sides:
        count = lax.axis_size(axis)
        forward = [(i, i + 1) for i in range(count - 1)]
        if periodic:
            forward.append((count - 1, 0))
        backward = [(target, source) for source, target in forward]
        low = lax.ppermute(
            lax.slice_in_dim(block, block.shape[dim] - width, None, axis=dim), axis, forward
        )
        high = lax.ppermute(lax.slice_in_dim(block, 0, width, axis=dim), axis, backward)
        block = jnp.concatenate([low, block, high], axis=dim)
    return block


def framed(field):
    tall = extended(field, (("lat", 1),), 1, False)
    return extended(tall, (("lon", 2),), 1, True)


def convolve(padded, kernel, stride, dilate, padding):
    return lax.conv_general_dilated(
        padded,
        kernel,
        (stride, stride),
        padding,
        lhs_dilation=(dilate, dilate),
        dimension_numbers=("NHWC", "HWIO", "NHWC"),
        preferred_element_type=jnp.float32,
    )


def taps_down(padded, kernel):
    return convolve(padded, kernel, 2, 1, "VALID")


def taps_same(padded, kernel):
    return convolve(padded, kernel, 1, 1, "VALID")


def taps_up(padded, kernel):
    return convolve(padded, kernel[::-1, ::-1], 1, 2, ((-1, 0), (-1, 0)))


def kernel_grad(padded, grad, dilate, layout):
    result = lax.conv_general_dilated(
        padded,
        grad,
        (1, 1),
        "VALID",
        rhs_dilation=(dilate, dilate),
        dimension_numbers=("CHWN", "IHWO", layout),
        preferred_element_type=jnp.float32,
    )
    return result[:3, :3]


def swap_io(kernel):
    return jnp.transpose(kernel, (0, 1, 3, 2))


def body(fields, down_weight, mid_weight, up_weight, cotangent):
    kernel_down, kernel_mid, kernel_up = (
        lax.all_gather(down_weight, "dp", axis=2, tiled=True),
        lax.all_gather(mid_weight, "dp", axis=2, tiled=True),
        lax.all_gather(up_weight, "dp", axis=2, tiled=True),
    )
    cells = (
        fields.shape[0]
        * lax.axis_size("dp")
        * fields.shape[1]
        * lax.axis_size("lat")
        * fields.shape[2]
        * lax.axis_size("lon")
    )
    scale = 1.0 / math.sqrt(cells)
    framed_in = framed(fields)
    down = taps_down(framed_in, kernel_down).astype(jnp.bfloat16)
    framed_down = framed(down)
    pre = taps_same(framed_down, kernel_mid)
    mid = jax.nn.silu(pre).astype(jnp.bfloat16)
    framed_mid = framed(mid)
    level_out = (fields.astype(jnp.float32) + taps_up(framed_mid, kernel_up)).astype(jnp.bfloat16)
    framed_cot = framed(cotangent)
    up_term = kernel_grad(framed_cot, mid, 2, "HWCN") * scale
    grad_mid_map = taps_down(framed_cot, swap_io(kernel_up))
    sig = jax.nn.sigmoid(pre)
    grad_pre = (grad_mid_map * sig * (1.0 + pre * (1.0 - sig))).astype(jnp.bfloat16)
    mid_term = kernel_grad(framed_down, grad_pre, 1, "HWNC") * scale
    grad_down_map = taps_same(framed(grad_pre), swap_io(kernel_mid)[::-1, ::-1]).astype(
        jnp.bfloat16
    )
    down_term = kernel_grad(framed_in, grad_down_map, 2, "HWNC") * scale
    grad_fields = (
        cotangent.astype(jnp.float32) + taps_up(framed(grad_down_map), swap_io(kernel_down))
    ).astype(jnp.bfloat16)
    totals = lax.psum((down_term, mid_term, up_term), ("lat", "lon"))
    grad_down, grad_mid, grad_up = (
        lax.psum_scatter(
            totals[0].astype(jnp.bfloat16), "dp", scatter_dimension=2, tiled=True
        ).astype(jnp.float32),
        lax.psum_scatter(
            totals[1].astype(jnp.bfloat16), "dp", scatter_dimension=2, tiled=True
        ).astype(jnp.float32),
        lax.psum_scatter(
            totals[2].astype(jnp.bfloat16), "dp", scatter_dimension=2, tiled=True
        ).astype(jnp.float32),
    )
    return (level_out, grad_fields, grad_down, grad_mid, grad_up)


def solution(mesh):
    in_specs = (
        P("dp", "lat", "lon", None),
        P(None, None, "dp", None),
        P(None, None, "dp", None),
        P(None, None, "dp", None),
        P("dp", "lat", "lon", None),
    )
    out_specs = (
        P("dp", "lat", "lon", None),
        P("dp", "lat", "lon", None),
        P(None, None, "dp", None),
        P(None, None, "dp", None),
        P(None, None, "dp", None),
    )
    return jax.shard_map(body, mesh=mesh, in_specs=in_specs, out_specs=out_specs, check_vma=False)
```

profile of v0, /device:TPU:16, one launch (start us, length us, event | category | flops | bytes accessed | tf_op | source)
XLA Modules:
  0.0 591.8 jit_solution(1721154471314080505)
XLA Ops:
  8.0 2.1 collective-permute-start.1
  10.2 6.1 %collective-permute-start = (bf16[1,1,128,128]{3,2,1,0:T(8,128)(2,1)S(1)}, bf16[1,1,128,128]{3,2,1,0:T(8,128)(2,1)S(1)}, u32[]{:S(2)}, u32[]{:S(2)}) collective-permute-start(bf16[1,1,128,128]{3,2,1,0:T(8,128)(2,1)S(1)} %get-tuple-element.33), channel_id=1, source_target_pairs={{0,8},{8,16},{16,24},{24,32},{32,40},{40,48},{48,56},{1,9},{9,17},... | collective-permute-start | bytes 98312 | tf_op jit(solution)/shard_map/ppermute | solution.py:15
  17.0 1.9 collective-permute-start.13
  18.9 6.3 %collective-permute-start.12 = (bf16[1,1,128,128]{3,2,1,0:T(8,128)(2,1)S(1)}, bf16[1,1,128,128]{3,2,1,0:T(8,128)(2,1)S(1)}, u32[]{:S(2)}, u32[]{:S(2)}) collective-permute-start(bf16[1,1,128,128]{3,2,1,0:T(8,128)(2,1)S(1)} %get-tuple-element.31), channel_id=1, source_target_pairs={{0,8},{8,16},{16,24},{24,32},{32,40},{40,48},{48,56},{1,9},{9,17},... | collective-permute-start | bytes 98312 | tf_op jit(solution)/shard_map/ppermute | solution.py:15
  25.3 2.3 all_gather.9
  27.6 3.7 all_gather.10
  31.3 3.9 all_gather.11
  35.2 2.4 constant_dynamic-update-slice_fusion.1
  39.6 2.6 collective-permute-start.3
  42.4 4.6 collective-permute-start.15
  47.0 1.7 maximum_bitcast_fusion
  51.5 1.9 select_convert_fusion.1
  53.5 1.7 maximum_bitcast_fusion.1
  58.7 1.8 slice.186
  61.5 2.4 collective-permute-start.4
  63.9 5.1 collective-permute-start.5
  69.1 4.4 fusion.132
  75.3 2.4 fusion.133
  77.7 1.9 fusion.41
  80.8 4.1 collective-permute-start.7
  84.9 1.9 fusion.38
  87.9 2.4 copy.61
  92.5 2.0 multiply_convert_fusion.1
  95.6 2.4 multiply_convert_fusion
  103.5 3.3 collective-permute-start.8
  106.8 4.6 collective-permute-start.9
  111.4 2.0 slice_bitcast_fusion.2
  114.1 3.6 collective-permute-start.16
  117.8 4.1 collective-permute-start.17
  123.1 5.3 fusion.79
  128.4 2.3 fusion.73
  131.0 4.1 collective-permute-start.19
  137.6 1.9 select_convert_fusion
  140.6 3.6 fusion.76
  144.2 346.6 %all-reduce.2 = (bf16[3,3,128,128]{3,2,1,0:T(8,128)(2,1)}, bf16[3,3,128,128]{3,2,1,0:T(8,128)(2,1)}, bf16[3,3,128,128]{3,2,1,0:T(8,128)(2,1)}) all-reduce(f32[3,3,128,128]{3,2,1,0:T(8,128)} %fusion.76, f32[3,3,128,128]{3,2,1,0:T(8,128)S(1)} %copy-done.25, ...), channel_id=1, replica_groups=mesh['dp'=2,'lat'=8,'lon'=8] {'lat','lon'}, use_global_device_ids=true, to_apply=%region_0.1 | all-reduce | flops 442368 | bytes 2654208 | tf_op jit(solution)/shard_map/psum | solution.py:104
  492.8 4.1 collective-permute-start.11
  498.3 1.9 collective-permute-start.20
  500.2 22.3 %collective-permute-start.21 = (bf16[1,1,64,128]{3,0,2,1:T(2,128)(2,1)S(1)}, bf16[1,1,64,128]{3,0,2,1:T(2,128)(2,1)S(1)}, u32[]{:S(2)}, u32[]{:S(2)}) collective-permute-start(bf16[1,1,64,128]{3,0,2,1:T(2,128)(2,1)S(1)} %slice.175), channel_id=1, source_target_pairs={{8,0},{16,8},{24,16},{32,24},{40,32},{48,40},{56,48},{9,1},{17,9},... | collective-permute-start | bytes 49160 | tf_op jit(solution)/shard_map/ppermute | solution.py:18
  522.7 3.7 pad_maximum_fusion.15
  529.1 3.2 collective-permute-start.23
  532.3 20.0 %fusion.21 = bf16[1,80,128,128]{3,0,2,1:T(2,128)(2,1)S(1)} fusion(bf16[1,80,128,128]{3,2,1,0:T(8,128)(2,1)S(1)} %copy-done.12, bf16[3,3,128,128]{3,2,1,0:T(8,128)(2,1)S(1)} %copy-done.29, bf16[1,42,66,128]{3,0,2,1:T(2,128)(2,1)S(1)} %pad_maximum_fusion.15), kind=kOutput, calls=%fused_computation.25 | convolution fusion | flops 758906880 | bytes 6247424 | tf_op jit(solution)/shard_map/conv_general_dilated | solution.py:29
  552.3 2.0 copy.78
  554.4 3.7 pad_maximum_fusion.14
  558.1 20.0 %fusion.19 = bf16[1,80,128,128]{3,0,2,1:T(2,128)(2,1)S(1)} fusion(bf16[1,80,128,128]{3,2,1,0:T(8,128)(2,1)S(1)} %copy-done.14, bf16[3,3,128,128]{3,2,1,0:T(8,128)(2,1)S(1)} %copy-done.27, bf16[1,42,66,128]{3,0,2,1:T(2,128)(2,1)S(1)} %pad_maximum_fusion.14), kind=kOutput, calls=%fused_computation.22 | convolution fusion | flops 758906880 | bytes 6247424 | tf_op jit(solution)/shard_map/conv_general_dilated | solution.py:29
  578.1 2.0 copy.79
  580.1 1.6 convert_element_type.55
  581.7 1.6 convert_element_type.53
  583.4 1.6 convert_element_type.51
  (189 shorter events, 35.5 us)
Async XLA Ops:
  7.2 572.9 %reduce-scatter.8.cloned.1.call-start = ((), (), s32[]{:S(2)}) async-start(), calls=%async_computation.5 | async-start | bytes 442368 | tf_op jit(solution)/shard_map/reduce_scatter | solution.py:112
  8.0 29.6 %collective-permute-start.1 = (bf16[1,1,128,128]{3,2,1,0:T(8,128)(2,1)S(1)}, bf16[1,1,128,128]{3,2,1,0:T(8,128)(2,1)S(1)}, u32[]{:S(2)}, u32[]{:S(2)}) collective-permute-start(bf16[1,1,128,128]{3,2,1,0:T(8,128)(2,1)S(1)} %get-tuple-element.32), channel_id=1, source_target_pairs={{8,0},{16,8},{24,16},{32,24},{40,32},{48,40},{56,48},{9,1},{17,9},... | collective-permute-start | bytes 98312 | tf_op jit(solution)/shard_map/ppermute | solution.py:18
  10.2 25.0 %collective-permute-start = (bf16[1,1,128,128]{3,2,1,0:T(8,128)(2,1)S(1)}, bf16[1,1,128,128]{3,2,1,0:T(8,128)(2,1)S(1)}, u32[]{:S(2)}, u32[]{:S(2)}) collective-permute-start(bf16[1,1,128,128]{3,2,1,0:T(8,128)(2,1)S(1)} %get-tuple-element.33), channel_id=1, source_target_pairs={{0,8},{8,16},{16,24},{24,32},{32,40},{40,48},{48,56},{1,9},{9,17},... | collective-permute-start | bytes 98312 | tf_op jit(solution)/shard_map/ppermute | solution.py:15
  17.0 25.2 %collective-permute-start.13 = (bf16[1,1,128,128]{3,2,1,0:T(8,128)(2,1)S(1)}, bf16[1,1,128,128]{3,2,1,0:T(8,128)(2,1)S(1)}, u32[]{:S(2)}, u32[]{:S(2)}) collective-permute-start(bf16[1,1,128,128]{3,2,1,0:T(8,128)(2,1)S(1)} %get-tuple-element.30), channel_id=1, source_target_pairs={{8,0},{16,8},{24,16},{32,24},{40,32},{48,40},{56,48},{9,1},{17,9},... | collective-permute-start | bytes 98312 | tf_op jit(solution)/shard_map/ppermute | solution.py:18
  18.9 18.7 %collective-permute-start.12 = (bf16[1,1,128,128]{3,2,1,0:T(8,128)(2,1)S(1)}, bf16[1,1,128,128]{3,2,1,0:T(8,128)(2,1)S(1)}, u32[]{:S(2)}, u32[]{:S(2)}) collective-permute-start(bf16[1,1,128,128]{3,2,1,0:T(8,128)(2,1)S(1)} %get-tuple-element.31), channel_id=1, source_target_pairs={{0,8},{8,16},{16,24},{24,32},{32,40},{40,48},{48,56},{1,9},{9,17},... | collective-permute-start | bytes 98312 | tf_op jit(solution)/shard_map/ppermute | solution.py:15
  27.6 23.9 %copy-start.26 = (bf16[3,3,128,128]{3,2,1,0:T(8,128)(2,1)}, bf16[3,3,128,128]{3,2,1,0:T(8,128)(2,1)S(1)}, u32[]{:S(2)}) copy-start(bf16[3,3,128,128]{3,2,1,0:T(8,128)(2,1)S(1)} %all_gather.9) | copy-start | bytes 884740
  38.0 8.9 %collective-permute-start.2 = (bf16[1,82,1,128]{3,2,1,0:T(2,128)(2,1)S(1)}, bf16[1,82,1,128]{3,2,1,0:T(2,128)(2,1)S(1)}, u32[]{:S(2)}, u32[]{:S(2)}) collective-permute-start(bf16[1,82,1,128]{3,2,1,0:T(2,128)(2,1)S(1)} %get-tuple-element.28), channel_id=1, source_target_pairs={{0,1},{1,2},{2,3},{3,4},{4,5},{5,6},{6,7},{7,0},{8,9},{9,10},{10,1... | collective-permute-start | bytes 62984 | tf_op jit(solution)/shard_map/ppermute | solution.py:15
  39.6 7.4 %collective-permute-start.3 = (bf16[1,82,1,128]{3,2,1,0:T(2,128)(2,1)S(1)}, bf16[1,82,1,128]{3,2,1,0:T(2,128)(2,1)S(1)}, u32[]{:S(2)}, u32[]{:S(2)}) collective-permute-start(bf16[1,82,1,128]{3,2,1,0:T(2,128)(2,1)S(1)} %get-tuple-element.29), channel_id=1, source_target_pairs={{1,0},{2,1},{3,2},{4,3},{5,4},{6,5},{7,6},{0,7},{9,8},{10,9},{11,1... | collective-permute-start | bytes 62984 | tf_op jit(solution)/shard_map/ppermute | solution.py:18
  42.3 11.2 %collective-permute-start.14 = (bf16[1,82,1,128]{3,2,1,0:T(2,128)(2,1)S(1)}, bf16[1,82,1,128]{3,2,1,0:T(2,128)(2,1)S(1)}, u32[]{:S(2)}, u32[]{:S(2)}) collective-permute-start(bf16[1,82,1,128]{3,2,1,0:T(2,128)(2,1)S(1)} %get-tuple-element.26), channel_id=1, source_target_pairs={{0,1},{1,2},{2,3},{3,4},{4,5},{5,6},{6,7},{7,0},{8,9},{9,10},{10,1... | collective-permute-start | bytes 62984 | tf_op jit(solution)/shard_map/ppermute | solution.py:15
  42.4 11.1 %collective-permute-start.15 = (bf16[1,82,1,128]{3,2,1,0:T(2,128)(2,1)S(1)}, bf16[1,82,1,128]{3,2,1,0:T(2,128)(2,1)S(1)}, u32[]{:S(2)}, u32[]{:S(2)}) collective-permute-start(bf16[1,82,1,128]{3,2,1,0:T(2,128)(2,1)S(1)} %get-tuple-element.27), channel_id=1, source_target_pairs={{1,0},{2,1},{3,2},{4,3},{5,4},{6,5},{7,6},{0,7},{9,8},{10,9},{11,1... | collective-permute-start | bytes 62984 | tf_op jit(solution)/shard_map/ppermute | solution.py:18
  50.4 3.0 copy-start.4
  57.8 2.7 copy-start.2
  61.5 18.3 %collective-permute-start.4 = (bf16[1,1,64,128]{3,2,1,0:T(8,128)(2,1)S(1)}, bf16[1,1,64,128]{3,2,1,0:T(8,128)(2,1)S(1)}, u32[]{:S(2)}, u32[]{:S(2)}) collective-permute-start(bf16[1,1,64,128]{3,2,1,0:T(8,128)(2,1)S(1)} %slice.150), channel_id=1, source_target_pairs={{0,8},{8,16},{16,24},{24,32},{32,40},{40,48},{48,56},{1,9},{9,17},... | collective-permute-start | bytes 49160 | tf_op jit(solution)/shard_map/ppermute | solution.py:15
  63.9 15.9 %collective-permute-start.5 = (bf16[1,1,64,128]{3,1,2,0:T(2,128)(2,1)S(1)}, bf16[1,1,64,128]{3,1,2,0:T(2,128)(2,1)S(1)}, u32[]{:S(2)}, u32[]{:S(2)}) collective-permute-start(bf16[1,1,64,128]{3,1,2,0:T(2,128)(2,1)S(1)} %slice.153), channel_id=1, source_target_pairs={{8,0},{16,8},{24,16},{32,24},{40,32},{48,40},{56,48},{9,1},{17,9},... | collective-permute-start | bytes 49160 | tf_op jit(solution)/shard_map/ppermute | solution.py:18
  79.6 5.3 copy-start.23
  80.7 10.4 %collective-permute-start.6 = (bf16[1,42,1,128]{3,1,2,0:T(8,128)(2,1)S(1)}, bf16[1,42,1,128]{3,1,2,0:T(8,128)(2,1)S(1)}, u32[]{:S(2)}, u32[]{:S(2)}) collective-permute-start(bf16[1,42,1,128]{3,1,2,0:T(8,128)(2,1)S(1)} %get-tuple-element.52), channel_id=1, source_target_pairs={{0,1},{1,2},{2,3},{3,4},{4,5},{5,6},{6,7},{7,0},{8,9},{9,10},{10,1... | collective-permute-start | bytes 32264 | tf_op jit(solution)/shard_map/ppermute | solution.py:15
  80.8 10.3 %collective-permute-start.7 = (bf16[1,42,1,128]{3,1,2,0:T(8,128)(2,1)S(1)}, bf16[1,42,1,128]{3,1,2,0:T(8,128)(2,1)S(1)}, u32[]{:S(2)}, u32[]{:S(2)}) collective-permute-start(bf16[1,42,1,128]{3,1,2,0:T(8,128)(2,1)S(1)} %get-tuple-element.53), channel_id=1, source_target_pairs={{1,0},{2,1},{3,2},{4,3},{5,4},{6,5},{7,6},{0,7},{9,8},{10,9},{11,1... | collective-permute-start | bytes 32264 | tf_op jit(solution)/shard_map/ppermute | solution.py:18
  84.9 2.9 copy-start.3
  92.5 3.1 copy-start.28
  94.5 3.5 copy-start.19
  98.0 4.1 copy-start.21
  103.5 31.6 %collective-permute-start.8 = (bf16[1,1,64,128]{3,0,2,1:T(2,128)(2,1)}, bf16[1,1,64,128]{3,0,2,1:T(2,128)(2,1)}, u32[]{:S(2)}, u32[]{:S(2)}) collective-permute-start(bf16[1,1,64,128]{3,0,2,1:T(2,128)(2,1)} %slice.156), channel_id=1, source_target_pairs={{0,8},{8,16},{16,24},{24,32},{32,40},{40,48},{48,56},{1,9},{9,17},... | collective-permute-start | bytes 49160 | tf_op jit(solution)/shard_map/ppermute | solution.py:15
  106.8 385.8 %collective-permute-start.9 = (bf16[1,1,64,128]{3,0,2,1:T(2,128)(2,1)}, bf16[1,1,64,128]{3,0,2,1:T(2,128)(2,1)S(1)}, u32[]{:S(2)}, u32[]{:S(2)}) collective-permute-start(bf16[1,1,64,128]{3,0,2,1:T(2,128)(2,1)} %slice.159), channel_id=1, source_target_pairs={{8,0},{16,8},{24,16},{32,24},{40,32},{48,40},{56,48},{9,1},{17,9},... | collective-permute-start | bytes 49160 | tf_op jit(solution)/shard_map/ppermute | solution.py:18
  114.1 16.7 %collective-permute-start.16 = (bf16[1,1,64,128]{3,2,1,0:T(8,128)(2,1)}, bf16[1,1,64,128]{3,2,1,0:T(8,128)(2,1)S(1)}, u32[]{:S(2)}, u32[]{:S(2)}) collective-permute-start(bf16[1,1,64,128]{3,2,1,0:T(8,128)(2,1)} %slice.166), channel_id=1, source_target_pairs={{0,8},{8,16},{16,24},{24,32},{32,40},{40,48},{48,56},{1,9},{9,17},... | collective-permute-start | bytes 49160 | tf_op jit(solution)/shard_map/ppermute | solution.py:15
  117.8 13.1 %collective-permute-start.17 = (bf16[1,1,64,128]{3,1,2,0:T(2,128)(2,1)S(1)}, bf16[1,1,64,128]{3,1,2,0:T(2,128)(2,1)S(1)}, u32[]{:S(2)}, u32[]{:S(2)}) collective-permute-start(bf16[1,1,64,128]{3,1,2,0:T(2,128)(2,1)S(1)} %slice.169), channel_id=1, source_target_pairs={{8,0},{16,8},{24,16},{32,24},{40,32},{48,40},{56,48},{9,1},{17,9},... | collective-permute-start | bytes 49160 | tf_op jit(solution)/shard_map/ppermute | solution.py:18
  123.1 5.3 copy-start.9
  123.1 5.3 copy-start.10
  123.1 5.3 copy-start.20
  130.9 5.9 collective-permute-start.18
  131.0 5.8 collective-permute-start.19
  136.8 2.7 copy-start.11
  137.5 3.1 copy-start.8
  139.5 357.5 %copy-start.22 = (bf16[40,8,9,128]{3,1,2,0:T(8,128)(2,1)}, bf16[40,8,9,128]{3,1,2,0:T(8,128)(2,1)S(1)}, u32[]{:S(2)}) copy-start(bf16[40,8,9,128]{3,1,2,0:T(8,128)(2,1)S(1)} %select_convert_fusion) | copy-start | bytes 2211844
  140.6 3.6 copy-start.25
  140.6 350.5 %copy-start.16 = (bf16[1,40,64,128]{3,1,2,0:T(8,128)(2,1)S(1)}, bf16[1,40,64,128]{3,1,2,0:T(8,128)(2,1)}, u32[]{:S(2)}) copy-start(bf16[1,40,64,128]{3,1,2,0:T(8,128)(2,1)} %slice_bitcast_fusion.2) | copy-start | bytes 1966084
  490.9 90.9 %reduce-scatter.6.cloned.1.call-start = ((), (), s32[]{:S(2)}) async-start(), calls=%async_computation.4 | async-start | bytes 442368 | tf_op jit(solution)/shard_map/reduce_scatter | solution.py:109
  492.6 29.9 %copy-start.17 = (bf16[1,42,64,128]{3,0,2,1:T(2,128)(2,1)}, bf16[1,42,64,128]{3,0,2,1:T(2,128)(2,1)S(1)}, u32[]{:S(2)}) copy-start(bf16[1,42,64,128]{3,0,2,1:T(2,128)(2,1)S(1)} %constant_dynamic-update-slice_fusion.3) | copy-start | bytes 2064388
  492.7 30.0 %collective-permute-start.10 = (bf16[1,42,1,128]{3,0,2,1:T(2,128)(2,1)S(1)}, bf16[1,42,1,128]{3,0,2,1:T(2,128)(2,1)}, u32[]{:S(2)}, u32[]{:S(2)}) collective-permute-start(bf16[1,42,1,128]{3,0,2,1:T(2,128)(2,1)S(1)} %get-tuple-element.36), channel_id=1, source_target_pairs={{0,1},{1,2},{2,3},{3,4},{4,5},{5,6},{6,7},{7,0},{8,9},{9,10},{10,1... | collective-permute-start | bytes 32264 | tf_op jit(solution)/shard_map/ppermute | solution.py:15
  492.8 29.9 %collective-permute-start.11 = (bf16[1,42,1,128]{3,0,2,1:T(2,128)(2,1)S(1)}, bf16[1,42,1,128]{3,0,2,1:T(2,128)(2,1)}, u32[]{:S(2)}, u32[]{:S(2)}) collective-permute-start(bf16[1,42,1,128]{3,0,2,1:T(2,128)(2,1)S(1)} %get-tuple-element.37), channel_id=1, source_target_pairs={{1,0},{2,1},{3,2},{4,3},{5,4},{6,5},{7,6},{0,7},{9,8},{10,9},{11,1... | collective-permute-start | bytes 32264 | tf_op jit(solution)/shard_map/ppermute | solution.py:18
  498.3 28.1 %collective-permute-start.20 = (bf16[1,1,64,128]{3,0,2,1:T(2,128)(2,1)S(1)}, bf16[1,1,64,128]{3,0,2,1:T(2,128)(2,1)S(1)}, u32[]{:S(2)}, u32[]{:S(2)}) collective-permute-start(bf16[1,1,64,128]{3,0,2,1:T(2,128)(2,1)S(1)} %slice.172), channel_id=1, source_target_pairs={{0,8},{8,16},{16,24},{24,32},{32,40},{40,48},{48,56},{1,9},{9,17},... | collective-permute-start | bytes 49160 | tf_op jit(solution)/shard_map/ppermute | solution.py:15
  500.2 27.7 %collective-permute-start.21 = (bf16[1,1,64,128]{3,0,2,1:T(2,128)(2,1)S(1)}, bf16[1,1,64,128]{3,0,2,1:T(2,128)(2,1)S(1)}, u32[]{:S(2)}, u32[]{:S(2)}) collective-permute-start(bf16[1,1,64,128]{3,0,2,1:T(2,128)(2,1)S(1)} %slice.175), channel_id=1, source_target_pairs={{8,0},{16,8},{24,16},{32,24},{40,32},{48,40},{56,48},{9,1},{17,9},... | collective-permute-start | bytes 49160 | tf_op jit(solution)/shard_map/ppermute | solution.py:18
  522.6 9.7 %copy-start.12 = (bf16[1,80,128,128]{3,2,1,0:T(8,128)(2,1)S(1)}, bf16[1,80,128,128]{3,2,1,0:T(8,128)(2,1)}, u32[]{:S(2)}) copy-start(bf16[1,80,128,128]{3,2,1,0:T(8,128)(2,1)} %param.5) | copy-start | bytes 7864324
  522.6 60.8 %reduce-scatter.4.cloned.1.call-start = ((), (), s32[]{:S(2)}) async-start(), calls=%async_computation.3 | async-start | bytes 442368 | tf_op jit(solution)/shard_map/reduce_scatter | solution.py:106
  522.7 9.6 %copy-start.29 = (bf16[3,3,128,128]{3,2,1,0:T(8,128)(2,1)S(1)}, bf16[3,3,128,128]{3,2,1,0:T(8,128)(2,1)}, u32[]{:S(2)}) copy-start(bf16[3,3,128,128]{3,2,1,0:T(8,128)(2,1)} %all_gather.11) | copy-start | bytes 884740
  528.1 26.3 %collective-permute-start.22 = (bf16[1,42,1,128]{3,0,2,1:T(2,128)(2,1)S(1)}, bf16[1,42,1,128]{3,0,2,1:T(2,128)(2,1)S(1)}, u32[]{:S(2)}, u32[]{:S(2)}) collective-permute-start(bf16[1,42,1,128]{3,0,2,1:T(2,128)(2,1)S(1)} %get-tuple-element.34), channel_id=1, source_target_pairs={{0,1},{1,2},{2,3},{3,4},{4,5},{5,6},{6,7},{7,0},{8,9},{9,10},{10,1... | collective-permute-start | bytes 32264 | tf_op jit(solution)/shard_map/ppermute | solution.py:15
  529.1 25.3 %collective-permute-start.23 = (bf16[1,42,1,128]{3,0,2,1:T(2,128)(2,1)S(1)}, bf16[1,42,1,128]{3,0,2,1:T(2,128)(2,1)S(1)}, u32[]{:S(2)}, u32[]{:S(2)}) collective-permute-start(bf16[1,42,1,128]{3,0,2,1:T(2,128)(2,1)S(1)} %get-tuple-element.35), channel_id=1, source_target_pairs={{1,0},{2,1},{3,2},{4,3},{5,4},{6,5},{7,6},{0,7},{9,8},{10,9},{11,1... | collective-permute-start | bytes 32264 | tf_op jit(solution)/shard_map/ppermute | solution.py:18
  554.3 3.7 copy-start.14
  554.3 3.7 copy-start.27
  (13 other events, 25.0 us)
Sparse Core Ops, SparseCore 0:
  491.0 25.6 reduce-scatter.7
  522.7 8.5 reduce-scatter.5
  554.5 6.6 reduce-scatter.3
where the time goes:
time: 596 us; the launch traced here: 592 us
  blocking collectives  357 us (60%)
  starting transfers between devices  88.9 us (15%)
  matrix products  59.4 us (10%)
  local copies, waits for them, and re-layouts  41.8 us (7%)
  other arithmetic  29.3 us (5%)
  between operations  14.9 us (2%)
    psum x1, blocking collectives, body(): totals = lax.psum((down_term, mid_term, up_term), ('lat', 'lon'))  347 us
    ppermute x12, starting transfers between devices, extended(): lax.ppermute(lax.slice_in_dim(block, 0, width, axis=dim), axis, backward)  63.1 us
    conv_general_dilated x6, matrix products, convolve(): lax.conv_general_dilated(padded, kernel, (stride, stride), padding, lhs_d...  48.2 us
    ppermute x12, starting transfers between devices, extended(): lax.ppermute(lax.slice_in_dim(block, block.shape[dim] - width, None, axis...  25.5 us
    concatenate x10, other arithmetic, extended(): block = jnp.concatenate([low, block, high], axis=dim)  17 us
    unnamed x76, local copies, waits for them, and re-layouts  16.7 us
    concatenate x22, local copies, waits for them, and re-layouts, extended(): block = jnp.concatenate([low, block, high], axis=dim)  12.3 us
  transfers between devices with their start and end apart: 27, of which 1 were waited for; matrix products, arithmetic and copies ran while one was open for 17% of the time, Pallas kernels for 0%

commit v1 on v0

--- a/solution.py
+++ b/solution.py
@@ -101,7 +101,7 @@
     grad_fields = (
         cotangent.astype(jnp.float32) + taps_up(framed(grad_down_map), swap_io(kernel_down))
     ).astype(jnp.bfloat16)
-    totals = lax.psum((down_term, mid_term, up_term), ("lat", "lon"))
+    totals = lax.psum(lax.psum((down_term, mid_term, up_term), "lat"), "lon")
     grad_down, grad_mid, grad_up = (
         lax.psum_scatter(
             totals[0].astype(jnp.bfloat16), "dp", scatter_dimension=2, tiled=True

time: 596 us -> 392 us (0.66)
  the two profiles are of different devices: /device:TPU:16 before, /device:TPU:0 now
where the time goes in v1:
time: 392 us; the launch traced here: 388 us
  waiting for transfers between devices  86.3 us (22%)
  blocking collectives  82.1 us (21%)
  starting transfers between devices  72.2 us (18%)
  matrix products  61.1 us (16%)
  local copies, waits for them, and re-layouts  44 us (11%)
  other arithmetic  27.8 us (7%)
  between operations  14.9 us (4%)
    psum x1, waiting for transfers between devices, body(): totals = lax.psum(lax.psum((down_term, mid_term, up_term), 'lat'), 'lon')  84.6 us
    psum x1, blocking collectives, body(): totals = lax.psum(lax.psum((down_term, mid_term, up_term), 'lat'), 'lon')  72.2 us
    conv_general_dilated x6, matrix products, convolve(): lax.conv_general_dilated(padded, kernel, (stride, stride), padding, lhs_d...  49.9 us
    ppermute x12, starting transfers between devices, extended(): lax.ppermute(lax.slice_in_dim(block, block.shape[dim] - width, None, axis...  39.9 us
    ppermute x12, starting transfers between devices, extended(): lax.ppermute(lax.slice_in_dim(block, 0, width, axis=dim), axis, backward)  32.1 us
    unnamed x72, local copies, waits for them, and re-layouts  18.5 us
    concatenate x10, other arithmetic, extended(): block = jnp.concatenate([low, block, high], axis=dim)  16.8 us
    concatenate x22, local copies, waits for them, and re-layouts, extended(): block = jnp.concatenate([low, block, high], axis=dim)  13 us
  transfers between devices with their start and end apart: 28, of which 2 were waited for; matrix products, arithmetic and copies ran while one was open for 27% of the time, Pallas kernels for 0%

profile of v1, /device:TPU:0, one launch (start us, length us, event | category | flops | bytes accessed | tf_op | source)
XLA Modules:
  0.0 388.3 jit_solution(17843596376590747179)
XLA Ops:
  9.3 6.1 %collective-permute-start = (bf16[1,1,128,128]{3,2,1,0:T(8,128)(2,1)S(1)}, bf16[1,1,128,128]{3,2,1,0:T(8,128)(2,1)S(1)}, u32[]{:S(2)}, u32[]{:S(2)}) collective-permute-start(bf16[1,1,128,128]{3,2,1,0:T(8,128)(2,1)S(1)} %get-tuple-element.36), channel_id=1, source_target_pairs={{0,8},{8,16},{16,24},{24,32},{32,40},{40,48},{48,56},{1,9},{9,17},... | collective-permute-start | bytes 98312 | tf_op jit(solution)/shard_map/ppermute | solution.py:15
  17.4 6.7 %collective-permute-start.12 = (bf16[1,1,128,128]{3,2,1,0:T(8,128)(2,1)S(1)}, bf16[1,1,128,128]{3,2,1,0:T(8,128)(2,1)S(1)}, u32[]{:S(2)}, u32[]{:S(2)}) collective-permute-start(bf16[1,1,128,128]{3,2,1,0:T(8,128)(2,1)S(1)} %get-tuple-element.34), channel_id=1, source_target_pairs={{0,8},{8,16},{16,24},{24,32},{32,40},{40,48},{48,56},{1,9},{9,17},... | collective-permute-start | bytes 98312 | tf_op jit(solution)/shard_map/ppermute | solution.py:15
  24.1 2.3 all_gather.9
  26.4 3.7 all_gather.10
  30.1 3.8 all_gather.11
  34.0 2.4 constant_dynamic-update-slice_fusion.1
  36.9 1.6 collective-permute-start.2
  38.4 2.6 collective-permute-start.3
  41.3 4.6 %collective-permute-start.15 = (bf16[1,82,1,128]{3,2,1,0:T(2,128)(2,1)S(1)}, bf16[1,82,1,128]{3,2,1,0:T(2,128)(2,1)S(1)}, u32[]{:S(2)}, u32[]{:S(2)}) collective-permute-start(bf16[1,82,1,128]{3,2,1,0:T(2,128)(2,1)S(1)} %get-tuple-element.30), channel_id=1, source_target_pairs={{1,0},{2,1},{3,2},{4,3},{5,4},{6,5},{7,6},{0,7},{9,8},{10,9},{11,1... | collective-permute-start | bytes 62984 | tf_op jit(solution)/shard_map/ppermute | solution.py:18
  45.8 1.7 maximum_bitcast_fusion
  50.3 1.9 select_convert_fusion.1
  52.4 1.7 maximum_bitcast_fusion.1
  57.6 1.8 slice.186
  60.4 6.3 %collective-permute-start.4 = (bf16[1,1,64,128]{3,2,1,0:T(8,128)(2,1)S(1)}, bf16[1,1,64,128]{3,2,1,0:T(8,128)(2,1)S(1)}, u32[]{:S(2)}, u32[]{:S(2)}) collective-permute-start(bf16[1,1,64,128]{3,2,1,0:T(8,128)(2,1)S(1)} %slice.150), channel_id=1, source_target_pairs={{0,8},{8,16},{16,24},{24,32},{32,40},{40,48},{48,56},{1,9},{9,17},... | collective-permute-start | bytes 49160 | tf_op jit(solution)/shard_map/ppermute | solution.py:15
  66.8 1.5 collective-permute-start.5
  68.3 4.3 %fusion.132 = (bf16[82,8,18,128,1]{3,1,4,2,0:T(8,128)(2,1)}, bf16[82,1,8,18,128]{4,2,3,0,1:T(8,128)(2,1)S(1)}) fusion(bf16[82,1,7,1,128]{4,2,3,0,1:T(8,128)(2,1)} %get-tuple-element.23, bf16[82,1,8,17,128]{4,2,3,0,1:T(8,128)(2,1)} %slice.186), kind=kLoop, calls=%fused_computation.152 | loop fusion | flops 9068544 | bytes 9047552 | tf_op jit(solution)/shard_map/concatenate | solution.py:19
  72.8 1.6 slice-done
  74.4 2.4 fusion.133
  76.8 1.9 fusion.41
  79.8 4.1 %collective-permute-start.7 = (bf16[1,42,1,128]{3,1,2,0:T(8,128)(2,1)S(1)}, bf16[1,42,1,128]{3,1,2,0:T(8,128)(2,1)S(1)}, u32[]{:S(2)}, u32[]{:S(2)}) collective-permute-start(bf16[1,42,1,128]{3,1,2,0:T(8,128)(2,1)S(1)} %get-tuple-element.56), channel_id=1, source_target_pairs={{1,0},{2,1},{3,2},{4,3},{5,4},{6,5},{7,6},{0,7},{9,8},{10,9},{11,1... | collective-permute-start | bytes 32264 | tf_op jit(solution)/shard_map/ppermute | solution.py:18
  84.0 1.9 fusion.38
  87.0 2.5 copy.61
  91.7 2.0 multiply_convert_fusion.1
  94.8 2.4 multiply_convert_fusion
  102.7 6.6 %collective-permute-start.8 = (bf16[1,1,64,128]{3,0,2,1:T(2,128)(2,1)}, bf16[1,1,64,128]{3,0,2,1:T(2,128)(2,1)}, u32[]{:S(2)}, u32[]{:S(2)}) collective-permute-start(bf16[1,1,64,128]{3,0,2,1:T(2,128)(2,1)} %slice.156), channel_id=1, source_target_pairs={{0,8},{8,16},{16,24},{24,32},{32,40},{40,48},{48,56},{1,9},{9,17},... | collective-permute-start | bytes 49160 | tf_op jit(solution)/shard_map/ppermute | solution.py:15
  111.3 6.0 %collective-permute-start.16 = (bf16[1,1,64,128]{3,2,1,0:T(8,128)(2,1)}, bf16[1,1,64,128]{3,2,1,0:T(8,128)(2,1)S(1)}, u32[]{:S(2)}, u32[]{:S(2)}) collective-permute-start(bf16[1,1,64,128]{3,2,1,0:T(8,128)(2,1)} %slice.166), channel_id=1, source_target_pairs={{0,8},{8,16},{16,24},{24,32},{32,40},{40,48},{48,56},{1,9},{9,17},... | collective-permute-start | bytes 49160 | tf_op jit(solution)/shard_map/ppermute | solution.py:15
  117.4 1.7 collective-permute-start.17
  120.3 5.3 %fusion.79 = f32[3,3,128,128]{3,2,1,0:T(8,128)} fusion(bf16[42,8,9,128,1]{3,1,4,2,0:T(8,128)(2,1)S(1)} %fusion.96, bf16[42,8,9,128,1]{3,1,4,2,0:T(8,128)(2,1)} %get-tuple-element.41, bf16[42,8,9,128,1]{3,1,4,2,0:T(8,128)(2,1)} %copy.67, bf16[40,8,9,128]{3,1,2,0:T(8,128)(2,1)} %copy-done.20, pred[8,9]{0,1:T(8,128)(4,1)S(1)} %copy-done.29), kind=kOutput, calls=%fused_computation.81 | convolution fusion | flops 852185088 | bytes 3649608 | tf_op jit(solution)/shard_map/conv_general_dilated | solution.py:53
  125.7 2.3 fusion.73
  128.2 4.1 %collective-permute-start.19 = (bf16[1,42,1,128]{3,1,2,0:T(8,128)(2,1)S(1)}, bf16[1,42,1,128]{3,1,2,0:T(8,128)(2,1)S(1)}, u32[]{:S(2)}, u32[]{:S(2)}) collective-permute-start(bf16[1,42,1,128]{3,1,2,0:T(8,128)(2,1)S(1)} %get-tuple-element.54), channel_id=1, source_target_pairs={{1,0},{2,1},{3,2},{4,3},{5,4},{6,5},{7,6},{0,7},{9,8},{10,9},{11,1... | collective-permute-start | bytes 32264 | tf_op jit(solution)/shard_map/ppermute | solution.py:18
  132.4 1.6 collective-permute-done.18
  134.8 1.9 select_convert_fusion
  137.8 3.6 fusion.76
  144.2 4.2 %collective-permute-start.11 = (bf16[1,42,1,128]{3,0,2,1:T(2,128)(2,1)S(1)}, bf16[1,42,1,128]{3,0,2,1:T(2,128)(2,1)S(1)}, u32[]{:S(2)}, u32[]{:S(2)}) collective-permute-start(bf16[1,42,1,128]{3,0,2,1:T(2,128)(2,1)S(1)} %get-tuple-element.40), channel_id=1, source_target_pairs={{1,0},{2,1},{3,2},{4,3},{5,4},{6,5},{7,6},{0,7},{9,8},{10,9},{11,1... | collective-permute-start | bytes 32264 | tf_op jit(solution)/shard_map/ppermute | solution.py:18
  149.8 6.1 %collective-permute-start.20 = (bf16[1,1,64,128]{3,0,2,1:T(2,128)(2,1)S(1)}, bf16[1,1,64,128]{3,0,2,1:T(2,128)(2,1)S(1)}, u32[]{:S(2)}, u32[]{:S(2)}) collective-permute-start(bf16[1,1,64,128]{3,0,2,1:T(2,128)(2,1)S(1)} %slice.172), channel_id=1, source_target_pairs={{0,8},{8,16},{16,24},{24,32},{32,40},{40,48},{48,56},{1,9},{9,17},... | collective-permute-start | bytes 49160 | tf_op jit(solution)/shard_map/ppermute | solution.py:15
  157.1 3.0 pad_maximum_fusion.15
  161.7 84.6 %all-reduce.5.cloned.1.call-done = (f32[3,3,128,128]{3,2,1,0:T(8,128)}, f32[3,3,128,128]{3,2,1,0:T(8,128)}, f32[3,3,128,128]{3,2,1,0:T(8,128)}) async-done(((f32[3,3,128,128]{3,2,1,0:T(8,128)}, f32[3,3,128,128]{3,2,1,0:T(8,128)}, f32[3,3,128,128]{3,2,1,0:T(8,128)}), (f32[3,3,128,128]{3,2,1,0:T(8,128)}, f32[3,3,128,128]{3,2,1,0:T(8,128)}, f32[3,3,128,128]{3,2,1,0:T(8,128)})) %all-reduce.5.cloned.1.call-update) | async-done | bytes 1769488 | tf_op jit(solution)/shard_map/psum | solution.py:104
  246.2 72.2 %all-reduce.6 = (bf16[3,3,128,128]{3,2,1,0:T(8,128)(2,1)}, bf16[3,3,128,128]{3,2,1,0:T(8,128)(2,1)}, bf16[3,3,128,128]{3,2,1,0:T(8,128)(2,1)}) all-reduce(f32[3,3,128,128]{3,2,1,0:T(8,128)} %get-tuple-element.18, f32[3,3,128,128]{3,2,1,0:T(8,128)} %get-tuple-element.19, ...), channel_id=1, replica_groups=mesh['dp'=2,'lat'=8,'lon'=8] {'lon'}, use_global_device_ids=true, to_apply=%region_1.2 | all-reduce | flops 442368 | bytes 2654208 | tf_op jit(solution)/shard_map/psum | solution.py:104
  318.6 3.6 copy_dynamic-update-slice_fusion
  323.7 4.1 %collective-permute-start.23 = (bf16[1,42,1,128]{3,0,2,1:T(2,128)(2,1)S(1)}, bf16[1,42,1,128]{3,0,2,1:T(2,128)(2,1)S(1)}, u32[]{:S(2)}, u32[]{:S(2)}) collective-permute-start(bf16[1,42,1,128]{3,0,2,1:T(2,128)(2,1)S(1)} %get-tuple-element.38), channel_id=1, source_target_pairs={{1,0},{2,1},{3,2},{4,3},{5,4},{6,5},{7,6},{0,7},{9,8},{10,9},{11,1... | collective-permute-start | bytes 32264 | tf_op jit(solution)/shard_map/ppermute | solution.py:18
  327.9 20.8 %fusion.21 = bf16[1,80,128,128]{3,0,2,1:T(2,128)(2,1)S(1)} fusion(bf16[1,80,128,128]{3,2,1,0:T(8,128)(2,1)S(1)} %copy-done.12, bf16[3,3,128,128]{3,2,1,0:T(8,128)(2,1)S(1)} %copy-done.27, bf16[1,42,66,128]{3,0,2,1:T(2,128)(2,1)} %pad_maximum_fusion.15), kind=kOutput, calls=%fused_computation.25 | convolution fusion | flops 758906880 | bytes 6247424 | tf_op jit(solution)/shard_map/conv_general_dilated | solution.py:29
  348.7 2.0 copy.78
  350.8 3.0 pad_maximum_fusion.14
  353.8 20.8 %fusion.19 = bf16[1,80,128,128]{3,0,2,1:T(2,128)(2,1)S(1)} fusion(bf16[1,80,128,128]{3,2,1,0:T(8,128)(2,1)S(1)} %copy-done.14, bf16[3,3,128,128]{3,2,1,0:T(8,128)(2,1)S(1)} %copy-done.25, bf16[1,42,66,128]{3,0,2,1:T(2,128)(2,1)} %pad_maximum_fusion.14), kind=kOutput, calls=%fused_computation.22 | convolution fusion | flops 758906880 | bytes 6247424 | tf_op jit(solution)/shard_map/conv_general_dilated | solution.py:29
  374.7 2.0 copy.79
  376.7 1.6 convert_element_type.55
  378.3 1.6 convert_element_type.53
  380.0 1.6 convert_element_type.51
  (188 shorter events, 37.2 us)
Async XLA Ops:
  7.2 239.1 %all-reduce.5.cloned.1.call-start = ((), (), s32[]{:S(2)}) async-start(), calls=%async_computation.6 | async-start | bytes 3538944 | tf_op jit(solution)/shard_map/psum | solution.py:104
  8.0 28.4 %collective-permute-start.1 = (bf16[1,1,128,128]{3,2,1,0:T(8,128)(2,1)S(1)}, bf16[1,1,128,128]{3,2,1,0:T(8,128)(2,1)S(1)}, u32[]{:S(2)}, u32[]{:S(2)}) collective-permute-start(bf16[1,1,128,128]{3,2,1,0:T(8,128)(2,1)S(1)} %get-tuple-element.35), channel_id=1, source_target_pairs={{8,0},{16,8},{24,16},{32,24},{40,32},{48,40},{56,48},{9,1},{17,9},... | collective-permute-start | bytes 98312 | tf_op jit(solution)/shard_map/ppermute | solution.py:18
  9.3 24.7 %collective-permute-start = (bf16[1,1,128,128]{3,2,1,0:T(8,128)(2,1)S(1)}, bf16[1,1,128,128]{3,2,1,0:T(8,128)(2,1)S(1)}, u32[]{:S(2)}, u32[]{:S(2)}) collective-permute-start(bf16[1,1,128,128]{3,2,1,0:T(8,128)(2,1)S(1)} %get-tuple-element.36), channel_id=1, source_target_pairs={{0,8},{8,16},{16,24},{24,32},{32,40},{40,48},{48,56},{1,9},{9,17},... | collective-permute-start | bytes 98312 | tf_op jit(solution)/shard_map/ppermute | solution.py:15
  16.1 25.0 %collective-permute-start.13 = (bf16[1,1,128,128]{3,2,1,0:T(8,128)(2,1)S(1)}, bf16[1,1,128,128]{3,2,1,0:T(8,128)(2,1)S(1)}, u32[]{:S(2)}, u32[]{:S(2)}) collective-permute-start(bf16[1,1,128,128]{3,2,1,0:T(8,128)(2,1)S(1)} %get-tuple-element.33), channel_id=1, source_target_pairs={{8,0},{16,8},{24,16},{32,24},{40,32},{48,40},{56,48},{9,1},{17,9},... | collective-permute-start | bytes 98312 | tf_op jit(solution)/shard_map/ppermute | solution.py:18
  17.4 19.1 %collective-permute-start.12 = (bf16[1,1,128,128]{3,2,1,0:T(8,128)(2,1)S(1)}, bf16[1,1,128,128]{3,2,1,0:T(8,128)(2,1)S(1)}, u32[]{:S(2)}, u32[]{:S(2)}) collective-permute-start(bf16[1,1,128,128]{3,2,1,0:T(8,128)(2,1)S(1)} %get-tuple-element.34), channel_id=1, source_target_pairs={{0,8},{8,16},{16,24},{24,32},{32,40},{40,48},{48,56},{1,9},{9,17},... | collective-permute-start | bytes 98312 | tf_op jit(solution)/shard_map/ppermute | solution.py:15
  26.4 23.9 %copy-start.24 = (bf16[3,3,128,128]{3,2,1,0:T(8,128)(2,1)}, bf16[3,3,128,128]{3,2,1,0:T(8,128)(2,1)S(1)}, u32[]{:S(2)}) copy-start(bf16[3,3,128,128]{3,2,1,0:T(8,128)(2,1)S(1)} %all_gather.9) | copy-start | bytes 884740
  36.9 8.9 %collective-permute-start.2 = (bf16[1,82,1,128]{3,2,1,0:T(2,128)(2,1)S(1)}, bf16[1,82,1,128]{3,2,1,0:T(2,128)(2,1)S(1)}, u32[]{:S(2)}, u32[]{:S(2)}) collective-permute-start(bf16[1,82,1,128]{3,2,1,0:T(2,128)(2,1)S(1)} %get-tuple-element.31), channel_id=1, source_target_pairs={{0,1},{1,2},{2,3},{3,4},{4,5},{5,6},{6,7},{7,0},{8,9},{9,10},{10,1... | collective-permute-start | bytes 62984 | tf_op jit(solution)/shard_map/ppermute | solution.py:15
  38.4 7.4 %collective-permute-start.3 = (bf16[1,82,1,128]{3,2,1,0:T(2,128)(2,1)S(1)}, bf16[1,82,1,128]{3,2,1,0:T(2,128)(2,1)S(1)}, u32[]{:S(2)}, u32[]{:S(2)}) collective-permute-start(bf16[1,82,1,128]{3,2,1,0:T(2,128)(2,1)S(1)} %get-tuple-element.32), channel_id=1, source_target_pairs={{1,0},{2,1},{3,2},{4,3},{5,4},{6,5},{7,6},{0,7},{9,8},{10,9},{11,1... | collective-permute-start | bytes 62984 | tf_op jit(solution)/shard_map/ppermute | solution.py:18
  41.2 11.2 %collective-permute-start.14 = (bf16[1,82,1,128]{3,2,1,0:T(2,128)(2,1)S(1)}, bf16[1,82,1,128]{3,2,1,0:T(2,128)(2,1)S(1)}, u32[]{:S(2)}, u32[]{:S(2)}) collective-permute-start(bf16[1,82,1,128]{3,2,1,0:T(2,128)(2,1)S(1)} %get-tuple-element.29), channel_id=1, source_target_pairs={{0,1},{1,2},{2,3},{3,4},{4,5},{5,6},{6,7},{7,0},{8,9},{9,10},{10,1... | collective-permute-start | bytes 62984 | tf_op jit(solution)/shard_map/ppermute | solution.py:15
  41.3 11.1 %collective-permute-start.15 = (bf16[1,82,1,128]{3,2,1,0:T(2,128)(2,1)S(1)}, bf16[1,82,1,128]{3,2,1,0:T(2,128)(2,1)S(1)}, u32[]{:S(2)}, u32[]{:S(2)}) collective-permute-start(bf16[1,82,1,128]{3,2,1,0:T(2,128)(2,1)S(1)} %get-tuple-element.30), channel_id=1, source_target_pairs={{1,0},{2,1},{3,2},{4,3},{5,4},{6,5},{7,6},{0,7},{9,8},{10,9},{11,1... | collective-permute-start | bytes 62984 | tf_op jit(solution)/shard_map/ppermute | solution.py:18
  49.3 3.0 copy-start.4
  56.7 2.8 copy-start.2
  60.4 18.5 %collective-permute-start.4 = (bf16[1,1,64,128]{3,2,1,0:T(8,128)(2,1)S(1)}, bf16[1,1,64,128]{3,2,1,0:T(8,128)(2,1)S(1)}, u32[]{:S(2)}, u32[]{:S(2)}) collective-permute-start(bf16[1,1,64,128]{3,2,1,0:T(8,128)(2,1)S(1)} %slice.150), channel_id=1, source_target_pairs={{0,8},{8,16},{16,24},{24,32},{32,40},{40,48},{48,56},{1,9},{9,17},... | collective-permute-start | bytes 49160 | tf_op jit(solution)/shard_map/ppermute | solution.py:15
  66.8 12.1 %collective-permute-start.5 = (bf16[1,1,64,128]{3,1,2,0:T(2,128)(2,1)S(1)}, bf16[1,1,64,128]{3,1,2,0:T(2,128)(2,1)S(1)}, u32[]{:S(2)}, u32[]{:S(2)}) collective-permute-start(bf16[1,1,64,128]{3,1,2,0:T(2,128)(2,1)S(1)} %slice.153), channel_id=1, source_target_pairs={{8,0},{16,8},{24,16},{32,24},{40,32},{48,40},{56,48},{9,1},{17,9},... | collective-permute-start | bytes 49160 | tf_op jit(solution)/shard_map/ppermute | solution.py:18
  78.6 5.3 %copy-start.22 = (bf16[82,1,7,1,128]{4,2,3,0,1:T(8,128)(2,1)S(1)}, bf16[82,1,7,1,128]{4,2,3,0,1:T(8,128)(2,1)}, u32[]{:S(2)}) copy-start(bf16[82,1,7,1,128]{4,2,3,0,1:T(8,128)(2,1)} %get-tuple-element.28) | copy-start | bytes 440836
  79.7 10.5 %collective-permute-start.6 = (bf16[1,42,1,128]{3,1,2,0:T(8,128)(2,1)S(1)}, bf16[1,42,1,128]{3,1,2,0:T(8,128)(2,1)S(1)}, u32[]{:S(2)}, u32[]{:S(2)}) collective-permute-start(bf16[1,42,1,128]{3,1,2,0:T(8,128)(2,1)S(1)} %get-tuple-element.55), channel_id=1, source_target_pairs={{0,1},{1,2},{2,3},{3,4},{4,5},{5,6},{6,7},{7,0},{8,9},{9,10},{10,1... | collective-permute-start | bytes 32264 | tf_op jit(solution)/shard_map/ppermute | solution.py:15
  79.8 10.5 %collective-permute-start.7 = (bf16[1,42,1,128]{3,1,2,0:T(8,128)(2,1)S(1)}, bf16[1,42,1,128]{3,1,2,0:T(8,128)(2,1)S(1)}, u32[]{:S(2)}, u32[]{:S(2)}) collective-permute-start(bf16[1,42,1,128]{3,1,2,0:T(8,128)(2,1)S(1)} %get-tuple-element.56), channel_id=1, source_target_pairs={{1,0},{2,1},{3,2},{4,3},{5,4},{6,5},{7,6},{0,7},{9,8},{10,9},{11,1... | collective-permute-start | bytes 32264 | tf_op jit(solution)/shard_map/ppermute | solution.py:18
  84.0 2.9 copy-start.3
  91.0 2.6 copy-start.6
  91.7 3.1 copy-start.26
  93.7 3.6 copy-start.18
  97.2 4.1 %copy-start.20 = (bf16[40,8,9,128]{3,1,2,0:T(8,128)(2,1)}, bf16[40,8,9,128]{3,1,2,0:T(8,128)(2,1)S(1)}, u32[]{:S(2)}) copy-start(bf16[40,8,9,128]{3,1,2,0:T(8,128)(2,1)S(1)} %multiply_convert_fusion) | copy-start | bytes 2211844
  102.7 38.8 %collective-permute-start.8 = (bf16[1,1,64,128]{3,0,2,1:T(2,128)(2,1)}, bf16[1,1,64,128]{3,0,2,1:T(2,128)(2,1)}, u32[]{:S(2)}, u32[]{:S(2)}) collective-permute-start(bf16[1,1,64,128]{3,0,2,1:T(2,128)(2,1)} %slice.156), channel_id=1, source_target_pairs={{0,8},{8,16},{16,24},{24,32},{32,40},{40,48},{48,56},{1,9},{9,17},... | collective-permute-start | bytes 49160 | tf_op jit(solution)/shard_map/ppermute | solution.py:15
  109.4 34.4 %collective-permute-start.9 = (bf16[1,1,64,128]{3,0,2,1:T(2,128)(2,1)}, bf16[1,1,64,128]{3,0,2,1:T(2,128)(2,1)S(1)}, u32[]{:S(2)}, u32[]{:S(2)}) collective-permute-start(bf16[1,1,64,128]{3,0,2,1:T(2,128)(2,1)} %slice.159), channel_id=1, source_target_pairs={{8,0},{16,8},{24,16},{32,24},{40,32},{48,40},{56,48},{9,1},{17,9},... | collective-permute-start | bytes 49160 | tf_op jit(solution)/shard_map/ppermute | solution.py:18
  111.3 16.7 %collective-permute-start.16 = (bf16[1,1,64,128]{3,2,1,0:T(8,128)(2,1)}, bf16[1,1,64,128]{3,2,1,0:T(8,128)(2,1)S(1)}, u32[]{:S(2)}, u32[]{:S(2)}) collective-permute-start(bf16[1,1,64,128]{3,2,1,0:T(8,128)(2,1)} %slice.166), channel_id=1, source_target_pairs={{0,8},{8,16},{16,24},{24,32},{32,40},{40,48},{48,56},{1,9},{9,17},... | collective-permute-start | bytes 49160 | tf_op jit(solution)/shard_map/ppermute | solution.py:15
  117.4 10.6 %collective-permute-start.17 = (bf16[1,1,64,128]{3,1,2,0:T(2,128)(2,1)S(1)}, bf16[1,1,64,128]{3,1,2,0:T(2,128)(2,1)S(1)}, u32[]{:S(2)}, u32[]{:S(2)}) collective-permute-start(bf16[1,1,64,128]{3,1,2,0:T(2,128)(2,1)S(1)} %slice.169), channel_id=1, source_target_pairs={{8,0},{16,8},{24,16},{32,24},{40,32},{48,40},{56,48},{9,1},{17,9},... | collective-permute-start | bytes 49160 | tf_op jit(solution)/shard_map/ppermute | solution.py:18
  120.3 5.3 %copy-start.9 = (bf16[82,8,18,128,1]{3,1,4,2,0:T(8,128)(2,1)S(1)}, bf16[82,8,18,128,1]{3,1,4,2,0:T(8,128)(2,1)}, u32[]{:S(2)}) copy-start(bf16[82,8,18,128,1]{3,1,4,2,0:T(8,128)(2,1)} %get-tuple-element.21) | copy-start | bytes 9068548
  120.3 5.3 %copy-start.10 = (bf16[82,8,18,128,1]{3,1,4,2,0:T(8,128)(2,1)S(1)}, bf16[82,8,18,128,1]{3,1,4,2,0:T(8,128)(2,1)}, u32[]{:S(2)}) copy-start(bf16[82,8,18,128,1]{3,1,4,2,0:T(8,128)(2,1)} %fusion.41) | copy-start | bytes 9068548
  120.3 5.3 %copy-start.19 = (bf16[40,8,9,128]{3,1,2,0:T(8,128)(2,1)S(1)}, bf16[40,8,9,128]{3,1,2,0:T(8,128)(2,1)}, u32[]{:S(2)}) copy-start(bf16[40,8,9,128]{3,1,2,0:T(8,128)(2,1)} %copy-done.18) | copy-start | bytes 2211844
  125.7 6.6 %copy-start.15 = (bf16[40,8,9,128]{3,0,2,1:T(8,128)(2,1)S(1)}, bf16[40,8,9,128]{3,0,2,1:T(8,128)(2,1)}, u32[]{:S(2)}) copy-start(bf16[40,8,9,128]{3,0,2,1:T(8,128)(2,1)} %copy.34) | copy-start | bytes 2211844
  128.1 5.9 %collective-permute-start.18 = (bf16[1,42,1,128]{3,1,2,0:T(8,128)(2,1)S(1)}, bf16[1,42,1,128]{3,1,2,0:T(8,128)(2,1)S(1)}, u32[]{:S(2)}, u32[]{:S(2)}) collective-permute-start(bf16[1,42,1,128]{3,1,2,0:T(8,128)(2,1)S(1)} %get-tuple-element.53), channel_id=1, source_target_pairs={{0,1},{1,2},{2,3},{3,4},{4,5},{5,6},{6,7},{7,0},{8,9},{9,10},{10,1... | collective-permute-start | bytes 32264 | tf_op jit(solution)/shard_map/ppermute | solution.py:15
  128.2 5.8 %collective-permute-start.19 = (bf16[1,42,1,128]{3,1,2,0:T(8,128)(2,1)S(1)}, bf16[1,42,1,128]{3,1,2,0:T(8,128)(2,1)S(1)}, u32[]{:S(2)}, u32[]{:S(2)}) collective-permute-start(bf16[1,42,1,128]{3,1,2,0:T(8,128)(2,1)S(1)} %get-tuple-element.54), channel_id=1, source_target_pairs={{1,0},{2,1},{3,2},{4,3},{5,4},{6,5},{7,6},{0,7},{9,8},{10,9},{11,1... | collective-permute-start | bytes 32264 | tf_op jit(solution)/shard_map/ppermute | solution.py:18
  134.0 2.7 copy-start.11
  134.8 3.1 copy-start.8
  136.7 11.7 %copy-start.21 = (bf16[40,8,9,128]{3,1,2,0:T(8,128)(2,1)}, bf16[40,8,9,128]{3,1,2,0:T(8,128)(2,1)S(1)}, u32[]{:S(2)}) copy-start(bf16[40,8,9,128]{3,1,2,0:T(8,128)(2,1)S(1)} %select_convert_fusion) | copy-start | bytes 2211844
  141.5 235.2 %reduce-scatter.8.cloned.1.call-start = ((), (), s32[]{:S(2)}) async-start(), calls=%async_computation.5 | async-start | bytes 442368 | tf_op jit(solution)/shard_map/reduce_scatter | solution.py:112
  143.9 13.2 %collective-permute-start.10 = (bf16[1,42,1,128]{3,0,2,1:T(2,128)(2,1)S(1)}, bf16[1,42,1,128]{3,0,2,1:T(2,128)(2,1)S(1)}, u32[]{:S(2)}, u32[]{:S(2)}) collective-permute-start(bf16[1,42,1,128]{3,0,2,1:T(2,128)(2,1)S(1)} %get-tuple-element.39), channel_id=1, source_target_pairs={{0,1},{1,2},{2,3},{3,4},{4,5},{5,6},{6,7},{7,0},{8,9},{9,10},{10,1... | collective-permute-start | bytes 32264 | tf_op jit(solution)/shard_map/ppermute | solution.py:15
  144.2 13.0 %collective-permute-start.11 = (bf16[1,42,1,128]{3,0,2,1:T(2,128)(2,1)S(1)}, bf16[1,42,1,128]{3,0,2,1:T(2,128)(2,1)S(1)}, u32[]{:S(2)}, u32[]{:S(2)}) collective-permute-start(bf16[1,42,1,128]{3,0,2,1:T(2,128)(2,1)S(1)} %get-tuple-element.40), channel_id=1, source_target_pairs={{1,0},{2,1},{3,2},{4,3},{5,4},{6,5},{7,6},{0,7},{9,8},{10,9},{11,1... | collective-permute-start | bytes 32264 | tf_op jit(solution)/shard_map/ppermute | solution.py:18
  149.8 11.3 %collective-permute-start.20 = (bf16[1,1,64,128]{3,0,2,1:T(2,128)(2,1)S(1)}, bf16[1,1,64,128]{3,0,2,1:T(2,128)(2,1)S(1)}, u32[]{:S(2)}, u32[]{:S(2)}) collective-permute-start(bf16[1,1,64,128]{3,0,2,1:T(2,128)(2,1)S(1)} %slice.172), channel_id=1, source_target_pairs={{0,8},{8,16},{16,24},{24,32},{32,40},{40,48},{48,56},{1,9},{9,17},... | collective-permute-start | bytes 49160 | tf_op jit(solution)/shard_map/ppermute | solution.py:15
  155.8 166.3 %collective-permute-start.21 = (bf16[1,1,64,128]{3,0,2,1:T(2,128)(2,1)S(1)}, bf16[1,1,64,128]{3,0,2,1:T(2,128)(2,1)S(1)}, u32[]{:S(2)}, u32[]{:S(2)}) collective-permute-start(bf16[1,1,64,128]{3,0,2,1:T(2,128)(2,1)S(1)} %slice.175), channel_id=1, source_target_pairs={{8,0},{16,8},{24,16},{32,24},{40,32},{48,40},{56,48},{9,1},{17,9},... | collective-permute-start | bytes 49160 | tf_op jit(solution)/shard_map/ppermute | solution.py:18
  160.1 167.7 %copy-start.12 = (bf16[1,80,128,128]{3,2,1,0:T(8,128)(2,1)S(1)}, bf16[1,80,128,128]{3,2,1,0:T(8,128)(2,1)}, u32[]{:S(2)}) copy-start(bf16[1,80,128,128]{3,2,1,0:T(8,128)(2,1)} %param.5) | copy-start | bytes 7864324
  161.0 166.8 %copy-start.27 = (bf16[3,3,128,128]{3,2,1,0:T(8,128)(2,1)S(1)}, bf16[3,3,128,128]{3,2,1,0:T(8,128)(2,1)}, u32[]{:S(2)}) copy-start(bf16[3,3,128,128]{3,2,1,0:T(8,128)(2,1)} %all_gather.11) | copy-start | bytes 884740
  318.5 59.8 %reduce-scatter.6.cloned.1.call-start = ((), (), s32[]{:S(2)}) async-start(), calls=%async_computation.4 | async-start | bytes 442368 | tf_op jit(solution)/shard_map/reduce_scatter | solution.py:109
  323.6 27.2 %collective-permute-start.22 = (bf16[1,42,1,128]{3,0,2,1:T(2,128)(2,1)S(1)}, bf16[1,42,1,128]{3,0,2,1:T(2,128)(2,1)S(1)}, u32[]{:S(2)}, u32[]{:S(2)}) collective-permute-start(bf16[1,42,1,128]{3,0,2,1:T(2,128)(2,1)S(1)} %get-tuple-element.37), channel_id=1, source_target_pairs={{0,1},{1,2},{2,3},{3,4},{4,5},{5,6},{6,7},{7,0},{8,9},{9,10},{10,1... | collective-permute-start | bytes 32264 | tf_op jit(solution)/shard_map/ppermute | solution.py:15
  323.7 27.1 %collective-permute-start.23 = (bf16[1,42,1,128]{3,0,2,1:T(2,128)(2,1)S(1)}, bf16[1,42,1,128]{3,0,2,1:T(2,128)(2,1)S(1)}, u32[]{:S(2)}, u32[]{:S(2)}) collective-permute-start(bf16[1,42,1,128]{3,0,2,1:T(2,128)(2,1)S(1)} %get-tuple-element.38), channel_id=1, source_target_pairs={{1,0},{2,1},{3,2},{4,3},{5,4},{6,5},{7,6},{0,7},{9,8},{10,9},{11,1... | collective-permute-start | bytes 32264 | tf_op jit(solution)/shard_map/ppermute | solution.py:18
  327.8 52.2 %reduce-scatter.4.cloned.1.call-start = ((), (), s32[]{:S(2)}) async-start(), calls=%async_computation.3 | async-start | bytes 442368 | tf_op jit(solution)/shard_map/reduce_scatter | solution.py:106
  350.7 3.0 copy-start.14
  350.7 3.1 copy-start.25
  (12 other events, 23.4 us)
Sparse Core Ops, SparseCore 0:
  141.6 104.5 all-reduce.4
  318.6 7.9 reduce-scatter.7
  329.6 11.7 reduce-scatter.5
  353.9 5.8 reduce-scatter.3
